TPU v7x, 512 devices: a whole 4x4x16 slice. The times are simulated.
512 devices in a mesh: seq: 64 (over z, x_lo, core), fsdp: 8 (over y, x_hi).
Axes of the slice: x: 4 (x_hi: 2, x_lo: 2; x = x_hi * 2 + x_lo), y: 4, z: 16, core: 2. Of those that a mesh axis runs over, the one named last changes fastest.
Arguments:
- q_s: bfloat16 [8, 64, 128, 1536], P('fsdp', 'seq'), may hold values from -48 to 48, as said below
- k_s: bfloat16 [8, 64, 128, 1536], P('fsdp', 'seq'), may hold values from -6 to 6, as said below
- v_s: bfloat16 [8, 64, 128, 1536], P('fsdp', 'seq'), may hold values from -6 to 6
- time_index: int32 [8], P('fsdp'), may hold values from 0 to 63
- ada_table: float32 [64, 2, 1536], replicated, may hold values from -3 to 3
- w_temporal: bfloat16 [1536, 4608], P('seq', 'fsdp'), may hold values from -0.15625 to 0.15625
Outputs:
- temporal_out: bfloat16 [8, 64, 128, 1536], P('fsdp', 'seq')
Inputs may be any that keep to these rules, and one draw needn't show every extreme that they name: `q_s`: real-valued entries. `k_s`: real-valued entries.
All inputs are finite; a program needn't handle non-finite values.
Results may differ from a plain program's by a relative error of at most 0.015.
Values may be sent and summed in bfloat16 or wider, within the bound.
No kernel may reach another device: no remote copies, remote signals or barrier semaphores. Data moves between devices by JAX's collectives and lax.ppermute only.
A program may use at most 64 MiB of HBM per device.

v0:
```python
import jax
import jax.numpy as jnp
from jax import lax
from jax.sharding import PartitionSpec as P

HEADS = 12
HEAD_SIZE = 128
ITERS = 3


relax_power = 0.8
norm_eps = 1e-06


def balanced_transport(logit_scores):
    potential_col = jnp.zeros_like(logit_scores[..., :1, :])
    potential_row = jnp.zeros_like(logit_scores[..., :, :1])
    for turn in range(ITERS):
        potential_row = -relax_power * jax.nn.logsumexp(
            logit_scores + potential_col, axis=-1, keepdims=True
        )
        potential_col = -relax_power * jax.nn.logsumexp(
            logit_scores + potential_row, axis=-2, keepdims=True
        )
    return jnp.exp(logit_scores + potential_row + potential_col).astype(jnp.bfloat16)


def temporal_attend(triple, logit_scale):
    temporal_logits = (
        jnp.einsum(
            "vfphd,vgphd->vphfg",
            triple[:, :, :, 0],
            triple[:, :, :, 1],
            preferred_element_type=jnp.float32,
        )
        * logit_scale
    )
    temporal_transport = balanced_transport(temporal_logits)
    temporal = jnp.einsum(
        "vphfg,vgphd->vfphd",
        temporal_transport,
        triple[:, :, :, 2],
        preferred_element_type=jnp.float32,
    )
    return temporal.astype(jnp.bfloat16)


def project(tokens, w_temporal):
    gathered = lax.all_gather(w_temporal, "fsdp", axis=1, tiled=True)
    whole = lax.all_gather(gathered, "seq", axis=0, tiled=True)
    return jnp.dot(tokens, whole, preferred_element_type=jnp.float32).astype(jnp.bfloat16)


def local(q_s, k_s, v_s, time_index, ada_table, w_temporal):
    positions = q_s.shape[2]
    width = HEADS * HEAD_SIZE
    logit_scale = 1.0 / HEAD_SIZE**0.5
    query_rows = q_s[0, 0].reshape(positions, HEADS, HEAD_SIZE)
    key_rows = k_s[0, 0].reshape(positions, HEADS, HEAD_SIZE)
    value_rows = v_s[0, 0].reshape(positions, HEADS, HEAD_SIZE)
    logit_scores = (
        jnp.einsum("pgl,bgl->gpb", query_rows, key_rows, preferred_element_type=jnp.float32)
        * logit_scale
    )
    transport_plan = balanced_transport(logit_scores)
    spatial_result = jnp.einsum(
        "bzg,gbq->zbq", transport_plan, value_rows, preferred_element_type=jnp.float32
    )
    spatial_result = spatial_result.reshape(positions, width).astype(jnp.bfloat16)
    selector = (jnp.arange(ada_table.shape[0]) == time_index[0]).astype(jnp.float32)
    modulate = jnp.einsum("t,tcw->cw", selector, ada_table, precision=lax.Precision.HIGHEST)
    hidden = spatial_result.astype(jnp.float32)
    scaled = hidden * lax.rsqrt(jnp.mean(hidden * hidden, axis=-1, keepdims=True) + norm_eps)
    modulated = (scaled * (1.0 + modulate[0]) + modulate[1]).astype(jnp.bfloat16)
    relayed = lax.all_to_all(modulated[None], "seq", split_axis=1, concat_axis=0, tiled=True)
    frames, local_pos = (relayed.shape[0], relayed.shape[1])
    triple = project(relayed.reshape(frames * local_pos, width), w_temporal)
    triple = triple.reshape(1, frames, local_pos, 3, HEADS, HEAD_SIZE)
    temporal = temporal_attend(triple, logit_scale).reshape(frames, local_pos, width)
    returned = lax.all_to_all(temporal, "seq", split_axis=0, concat_axis=1, tiled=True)
    return returned[None]


def solution(mesh):
    in_specs = (
        P("fsdp", "seq", None, None),
        P("fsdp", "seq", None, None),
        P("fsdp", "seq", None, None),
        P("fsdp"),
        P(),
        P("seq", "fsdp"),
    )
    out_specs = P("fsdp", "seq", None, None)
    return jax.shard_map(local, mesh=mesh, in_specs=in_specs, out_specs=out_specs, check_vma=False)
```

profile of v0, /device:TPU:1, one launch (start us, length us, event | category | flops | bytes accessed | tf_op | source)
XLA Modules:
  0.0 256.5 jit_solution(9671927672942869763)
XLA Ops:
  6.5 0.0 copy-start
  6.5 0.0 copy-start.1
  6.5 0.0 copy-start.2
  6.5 0.0 all-gather.3.cloned.1.call-start
  6.5 30.9 %all-gather = bf16[8,576,24]{1,2,0:T(8,128)(2,1)S(1)} all-gather(bf16[1,576,24]{1,2,0:T(8,128)(2,1)} %bitcast.56), channel_id=1, replica_groups=mesh['seq'=64,'fsdp'=8] {'fsdp'}, dimensions={0}, use_global_device_ids=true | all-gather | bytes 248832 | tf_op jit(solution)/shard_map/all_gather | solution.py:49
  37.5 0.9 reshape.479
  38.4 0.0 all-gather.3.cloned.1.call-update
  38.4 1.2 copy.71
  39.6 0.0 copy-done.1
  39.7 0.2 copy.72
  39.9 0.0 copy-done.2
  39.9 0.2 copy.75
  40.1 0.5 fusion.16
  40.6 0.5 exponential_reduce_fusion.11
  41.2 0.3 add_reduce_fusion.7
  41.5 0.3 exponential_reduce_fusion.10
  41.8 0.3 add_reduce_fusion.6
  42.1 0.5 exponential_reduce_fusion.9
  42.6 0.3 add_reduce_fusion.5
  42.9 0.3 exponential_reduce_fusion.8
  43.2 0.3 add_reduce_fusion.4
  43.5 0.5 exponential_reduce_fusion.7
  44.1 0.3 add_reduce_fusion.9
  44.4 0.3 exponential_reduce_fusion.6
  44.7 0.5 multiply_reduce_fusion
  45.1 0.3 copy.76
  46.1 0.0 copy-done
  46.1 0.4 fusion.2
  46.6 0.2 add_convert_fusion
  46.7 0.6 copy.113
  47.3 0.5 broadcast.318
  47.9 3.0 %reduce.30 = bf16[128,1536]{1,0:T(8,128)(2,1)S(1)} reduce(bf16[128,1,1536]{2,1,0:T(2,128)(2,1)S(1)} %bitcast.49, bf16[]{:T(256)} %broadcast.318), dimensions={1}, to_apply=%bitcast.46.reduce_sub_computation | reduce | bytes 786434
  50.9 0.1 reshape.485
  51.0 54.3 %all_to_all.8 = bf16[64,2,1536]{2,1,0:T(2,128)(2,1)S(1)} all-to-all(bf16[64,2,1536]{2,1,0:T(2,128)(2,1)S(1)} %reshape.485), channel_id=1, replica_groups=mesh['seq'=64,'fsdp'=8] {'seq'}, dimensions={0} | all-to-all | bytes 786432 | tf_op jit(solution)/shard_map/all_to_all | solution.py:75
  105.3 0.3 reshape.486
  105.7 93.0 %all-gather.3.cloned.1.call-done = bf16[1536,4608]{1,0:T(8,128)(2,1)} async-done(((bf16[24,4608]{1,0:T(8,128)(2,1)}), bf16[1536,4608]{1,0:T(8,128)(2,1)}) %all-gather.3.cloned.1.call-update) | async-done | bytes 14155792 | tf_op jit(solution)/shard_map/all_gather | solution.py:50
  198.7 7.0 %convolution_convert_fusion = bf16[128,4608]{1,0:T(8,128)(2,1)S(1)} fusion(bf16[1536,4608]{1,0:T(8,128)(2,1)} %all-gather.3.cloned.1.call-done, bf16[1,128,1536]{2,0,1:T(2,128)(2,1)S(1)} %bitcast.50), kind=kOutput, calls=%fused_computation | convolution fusion | flops 1812529152 | bytes 15728640 | tf_op jit(solution)/shard_map/dot_general | solution.py:51
  205.7 0.9 reshape.472
  206.6 0.3 fusion.15
  206.9 0.5 fusion.17
  207.3 0.5 exponential_reduce_fusion.5
  207.9 0.3 add_reduce_fusion.3
  208.2 0.3 exponential_reduce_fusion.4
  208.5 0.3 add_reduce_fusion.2
  208.8 0.5 exponential_reduce_fusion.3
  209.4 0.3 add_reduce_fusion.1
  209.7 0.3 exponential_reduce_fusion.2
  210.0 0.3 add_reduce_fusion
  210.3 0.5 exponential_reduce_fusion.1
  210.8 0.3 add_reduce_fusion.8
  211.1 0.3 exponential_reduce_fusion
  211.5 0.4 fusion.1
  211.9 0.3 copy.88
  212.2 0.2 reshape.482
  212.4 36.4 %all_to_all.9 = bf16[64,2,1536]{2,1,0:T(2,128)(2,1)S(1)} all-to-all(bf16[64,2,1536]{2,1,0:T(2,128)(2,1)S(1)} %reshape.482), channel_id=1, replica_groups=mesh['seq'=64,'fsdp'=8] {'seq'}, dimensions={0} | all-to-all | bytes 786432 | tf_op jit(solution)/shard_map/all_to_all | solution.py:80
  248.8 0.9 broadcast_in_dim.2
  (28 shorter events, 0.3 us)
Async XLA Ops:
  6.5 39.5 %copy-start = (f32[64,2,1536]{2,1,0:T(2,128)S(1)}, f32[64,2,1536]{2,1,0:T(2,128)}, u32[]{:S(2)}) copy-start(f32[64,2,1536]{2,1,0:T(2,128)} %param.10) | copy-start | bytes 2359300
  6.5 33.1 %copy-start.1 = (bf16[1,1,128,1536]{3,2,1,0:T(8,128)(2,1)S(1)}, bf16[1,1,128,1536]{3,2,1,0:T(8,128)(2,1)}, u32[]{:S(2)}) copy-start(bf16[1,1,128,1536]{3,2,1,0:T(8,128)(2,1)} %param.7) | copy-start | bytes 1179652
  6.5 33.3 %copy-start.2 = (bf16[1,1,128,1536]{3,2,1,0:T(8,128)(2,1)S(1)}, bf16[1,1,128,1536]{3,2,1,0:T(8,128)(2,1)}, u32[]{:S(2)}) copy-start(bf16[1,1,128,1536]{3,2,1,0:T(8,128)(2,1)} %param.8) | copy-start | bytes 1179652
  6.5 192.1 %all-gather.3.cloned.1.call-start = ((), (), s32[]{:S(2)}) async-start(), calls=%async_computation.2 | async-start | bytes 14376960 | tf_op jit(solution)/shard_map/all_gather | solution.py:50
Sparse Core Ops, SparseCore 0:
  38.5 160.0 all-gather.2
where the time goes:
time: 257 us
  blocking collectives  122 us (47%)
  waiting for transfers between devices  93 us (36%)
  between operations  14.5 us (6%)
  other arithmetic  11 us (4%)
  matrix products  9.32 us (4%)
  local copies, waits for them, and re-layouts  6.94 us (3%)
    all_gather x1, waiting for transfers between devices, project(): whole = lax.all_gather(gathered, 'seq', axis=0, tiled=True)  93 us
    all_to_all x1, blocking collectives, local(): lax.all_to_all(modulated[None], 'seq', split_axis=1, concat_axis=0, tiled...  54.3 us
    all_to_all x1, blocking collectives, local(): lax.all_to_all(temporal, 'seq', split_axis=0, concat_axis=1, tiled=True)  36.4 us
    all_gather x1, blocking collectives, project(): gathered = lax.all_gather(w_temporal, 'fsdp', axis=1, tiled=True)  30.9 us
    dot_general x1, matrix products, project(): jnp.dot(tokens, whole, preferred_element_type=jnp.float32)  7.04 us
  transfers between devices with their start and end apart: 1, of which 1 were waited for; matrix products, arithmetic and copies ran while one was open for 5% of the time, Pallas kernels for 0%

commit v1 on v0

v1 whole, which is shorter than its diff:
```python
import functools
import jax
import jax.numpy as jnp
from jax import lax
from jax.experimental import pallas as pl
from jax.experimental.pallas import tpu as pltpu
from jax.sharding import Mesh, PartitionSpec as P
HEADS=12; HEAD_SIZE=128; ITERS=3; POWER=0.8; EPS=1e-6

def transport(scores):
    col = None
    for _ in range(ITERS):
        shifted = scores if col is None else scores + col
        top = jnp.max(shifted, axis=-1, keepdims=True)
        row = -POWER * (top + jnp.log(jnp.sum(jnp.exp(shifted - top), axis=-1, keepdims=True)))
        shifted = scores + row
        top = jnp.max(shifted, axis=-2, keepdims=True)
        col = -POWER * (top + jnp.log(jnp.sum(jnp.exp(shifted - top), axis=-2, keepdims=True)))
    return jnp.exp(shifted + col).astype(jnp.bfloat16)

def spatial_kernel(group, idx_ref, q_ref, k_ref, v_ref, ada_ref, o_ref, acc_ref):
    step = pl.program_id(0)
    scale = 1.0 / HEAD_SIZE**0.5
    scores = []
    for h in range(group):
        lanes = slice(h*HEAD_SIZE,(h+1)*HEAD_SIZE)
        scores.append(lax.dot_general(q_ref[0,0,:,lanes], k_ref[0,0,:,lanes], (((1,),(1,)),((),())), preferred_element_type=jnp.float32)*scale)
    plan = transport(jnp.stack(scores))
    for h in range(group):
        lanes = slice(h*HEAD_SIZE,(h+1)*HEAD_SIZE)
        out = jnp.dot(plan[h], v_ref[0,0,:,lanes], preferred_element_type=jnp.float32).astype(jnp.bfloat16)
        acc_ref[step, :, lanes] = out
    @pl.when(step == pl.num_programs(0)-1)
    def _():
        n = HEADS//group
        total = None
        for s in range(n):
            part = acc_ref[s].astype(jnp.float32)
            part = jnp.sum(part*part, axis=-1, keepdims=True)
            total = part if total is None else total + part
        inv = lax.rsqrt(total/(HEADS*HEAD_SIZE) + EPS)
        w = group*HEAD_SIZE
        for s in range(n):
            part = acc_ref[s].astype(jnp.float32)
            o_ref[:, s*w:(s+1)*w] = (part*inv*(1.0+ada_ref[0,0:1,s*w:(s+1)*w])+ada_ref[0,1:2,s*w:(s+1)*w]).astype(jnp.bfloat16)

def spatial(idx, q, k, v, ada, group=3):
    width=HEADS*HEAD_SIZE; pos=q.shape[2]
    blk = pl.BlockSpec((1,1,pos,group*HEAD_SIZE), lambda i, idx: (0,0,0,i))
    return pl.pallas_call(
        functools.partial(spatial_kernel, group),
        out_shape=jax.ShapeDtypeStruct((pos,width), jnp.bfloat16),
        grid_spec=pltpu.PrefetchScalarGridSpec(
            num_scalar_prefetch=1, grid=(HEADS//group,),
            in_specs=[blk,blk,blk,pl.BlockSpec((1,2,width), lambda i, idx: (idx[0],0,0))],
            out_specs=pl.BlockSpec((pos,width), lambda i, idx: (0,0)),
            scratch_shapes=[pltpu.VMEM((HEADS//group,pos,group*HEAD_SIZE), jnp.bfloat16)]),
        compiler_params=pltpu.CompilerParams(dimension_semantics=("arbitrary",)),
        cost_estimate=pl.CostEstimate(flops=2*2*12*128*128*128, transcendentals=12*7*128*128, bytes_accessed=4*128*1536*2),
        name="spatial",
    )(idx, q, k, v, ada)

def temporal_kernel(heads, positions, x_ref, w_ref, o_ref):
    scale = 1.0 / HEAD_SIZE**0.5
    width = heads*HEAD_SIZE
    triple = jnp.dot(x_ref[0], w_ref[...], preferred_element_type=jnp.float32).astype(jnp.bfloat16)
    n = triple.shape[0]
    same = (lax.broadcasted_iota(jnp.int32,(n,n),0) % positions) == (lax.broadcasted_iota(jnp.int32,(n,n),1) % positions)
    scores=[]
    for h in range(heads):
        q = triple[:, h*HEAD_SIZE:(h+1)*HEAD_SIZE]
        k = triple[:, width+h*HEAD_SIZE:width+(h+1)*HEAD_SIZE]
        s = lax.dot_general(q,k,(((1,),(1,)),((),())),preferred_element_type=jnp.float32)*scale
        scores.append(jnp.where(same, s, -1e30))
    plan = transport(jnp.stack(scores))
    for h in range(heads):
        v = triple[:, 2*width+h*HEAD_SIZE:2*width+(h+1)*HEAD_SIZE]
        o_ref[0,:,h*HEAD_SIZE:(h+1)*HEAD_SIZE] = jnp.dot(plan[h], v, preferred_element_type=jnp.float32).astype(jnp.bfloat16)

def temporal(x, w, heads, positions):
    vids,n,width=x.shape
    return pl.pallas_call(
        functools.partial(temporal_kernel, heads, positions),
        out_shape=jax.ShapeDtypeStruct((vids,n,heads*HEAD_SIZE), jnp.bfloat16),
        grid=(vids,),
        in_specs=[pl.BlockSpec((1,n,width), lambda i:(i,0,0)), pl.BlockSpec(w.shape, lambda i:(0,0))],
        out_specs=pl.BlockSpec((1,n,heads*HEAD_SIZE), lambda i:(i,0,0)),
        compiler_params=pltpu.CompilerParams(dimension_semantics=("arbitrary",)),
        cost_estimate=pl.CostEstimate(flops=2*vids*n*width*3*heads*HEAD_SIZE, transcendentals=12*7*128*128, bytes_accessed=6*1024*1024),
        name="temporal",
    )(x, w)


UNIT = 192
PIECES = 3


def gather_weights(w):
    rows = w.shape[0]
    source = lax.axis_index("y") * 2 + lax.axis_index("xh")
    units = w.reshape(rows, PIECES, UNIT).transpose(1, 0, 2)
    ring = jnp.concatenate([units, jnp.zeros((8 - PIECES, rows, UNIT), w.dtype)], axis=0)
    ring = jnp.concatenate([ring, ring], axis=0)
    slots = lax.dynamic_slice_in_dim(ring, (-PIECES * source) % 8, 8, axis=0)
    slots = slots.reshape(1, 4, 1, 2, rows, UNIT)
    slots = jnp.broadcast_to(slots, (4, 4, 2, 2, rows, UNIT)).reshape(32, 2, rows, UNIT)
    slots = lax.all_to_all(slots, ("xl", "c", "y", "xh"), split_axis=0, concat_axis=0, tiled=True)
    slots = slots.reshape(2, 2, 8, 2, rows, UNIT)
    mine = lax.dynamic_index_in_dim(slots, lax.axis_index("c"), 0, keepdims=False)
    target = 2 * lax.axis_index("y")
    columns = []
    for part in range(3):
        for half in range(2):
            owner = (target + half + 8 * part) // PIECES
            columns.append(lax.dynamic_index_in_dim(mine[:, :, half], owner, 1, keepdims=False))
    block = jnp.concatenate(columns, axis=-1).reshape(2 * rows, 6 * UNIT)
    return lax.all_gather(block, ("z", "c"), axis=0, tiled=True)


def local(q_s, k_s, v_s, time_index, ada_table, w_temporal):
    width = HEADS * HEAD_SIZE
    weights = gather_weights(w_temporal)
    modulated = spatial(time_index, q_s, k_s, v_s, ada_table, 6)
    relayed = lax.all_to_all(modulated.reshape(64, 2, width), ("z", "xl", "c"), split_axis=0, concat_axis=0, tiled=True)
    relayed = jnp.broadcast_to(relayed.reshape(1, 128, width), (4, 128, width))
    tokens = lax.all_to_all(relayed, "y", split_axis=0, concat_axis=0, tiled=True)
    out = temporal(tokens, weights, 3, 2)
    out = out.reshape(4, 64, 2, 384).transpose(1, 0, 2, 3).reshape(256, 2, 384)
    out = lax.all_to_all(out, ("z", "xl", "c", "y"), split_axis=0, concat_axis=0, tiled=True)
    out = out.reshape(64, 4, 2, 384).transpose(0, 2, 1, 3)
    return out.reshape(1, 1, 128, width)


def solution(mesh):
    fine = Mesh(mesh.devices.reshape(16, 2, 2, 4, 2), ("z", "xl", "c", "y", "xh"))
    seq, fsdp = ("z", "xl", "c"), ("y", "xh")
    frames = P(fsdp, seq, None, None)
    in_specs = (frames, frames, frames, P(fsdp), P(), P(seq, fsdp))
    return jax.shard_map(local, mesh=fine, in_specs=in_specs, out_specs=frames, check_vma=False)
```

time: 257 us -> 179 us (0.70)
  waiting for transfers between devices: 93 us -> 22.9 us
  Pallas kernels: 0 us -> 14.1 us
  blocking collectives: 122 us -> 110 us
  other arithmetic: 11 us -> 0.13 us
  starting transfers between devices: 0.01 us -> 10.5 us
  matrix products: 9.32 us -> 0 us
    all_gather x1, waiting for transfers between devices: 93 us -> 8.58 us  [gather_weights(): return lax.all_gather(block, ('z', 'c'), axis=0, tiled=True)]
    all_gather x1 -> x0, blocking collectives: 30.9 us -> none  [project(): gathered = lax.all_gather(w_temporal, 'fsdp', axis=1, tiled=True)]
    all_to_all x2 -> x3, blocking collectives: 90.7 us -> 110 us  [the longest x1 44.6 us: local(): lax.all_to_all(modulated.reshape(64, 2, width), ('z', 'xl', 'c'), split_a...]
    all_to_all x0 -> x1, waiting for transfers between devices: none -> 14.3 us  [gather_weights(): lax.all_to_all(slots, ('xl', 'c', 'y', 'xh'), split_axis=0, concat_axis=0...]
    pallas_call x0 -> x2, Pallas kernels: none -> 14.1 us  [the longest x1 9.21 us: temporal(): pl.pallas_call(functools.partial(temporal_kernel, heads, positions), out_...]
    all_to_all x0 -> x1, starting transfers between devices: none -> 10.4 us  [gather_weights(): lax.all_to_all(slots, ('xl', 'c', 'y', 'xh'), split_axis=0, concat_axis=0...]
    dot_general x6 -> x0, matrix products: 9.32 us -> none  [the longest x1 7.04 us: project(): jnp.dot(tokens, whole, preferred_element_type=jnp.float32)]
    reduce_sum x12 -> x0, other arithmetic: 4.9 us -> none  [the longest x6 3.14 us: balanced_transport(): jax.nn.logsumexp(logit_scores + potential_col, axis=-1, keepdims=True)]
  transfers between devices with their start and end apart: 1 -> 2, of which waited for: 1 -> 2; matrix products, arithmetic and copies ran while one was open for 5% -> 1% of each run, Pallas kernels for 0% -> 3%
where the time goes in v1:
time: 179 us; the launch traced here: 178 us
  blocking collectives  110 us (61%)
  waiting for transfers between devices  22.9 us (13%)
  between operations  14.2 us (8%)
  Pallas kernels  14.1 us (8%)
  starting transfers between devices  10.5 us (6%)
  local copies, waits for them, and re-layouts  6.55 us (4%)
    all_to_all x1, blocking collectives, local(): lax.all_to_all(modulated.reshape(64, 2, width), ('z', 'xl', 'c'), split_a...  44.6 us
    all_to_all x1, blocking collectives, local(): lax.all_to_all(out, ('z', 'xl', 'c', 'y'), split_axis=0, concat_axis=0, t...  42.8 us
    all_to_all x1, blocking collectives, local(): lax.all_to_all(relayed, 'y', split_axis=0, concat_axis=0, tiled=True)  22.3 us
    all_to_all x1, waiting for transfers between devices, gather_weights(): lax.all_to_all(slots, ('xl', 'c', 'y', 'xh'), split_axis=0, concat_axis=0...  14.3 us
    all_to_all x1, starting transfers between devices, gather_weights(): lax.all_to_all(slots, ('xl', 'c', 'y', 'xh'), split_axis=0, concat_axis=0...  10.4 us
    pallas_call x1, Pallas kernels, temporal(): pl.pallas_call(functools.partial(temporal_kernel, heads, positions), out_...  9.21 us
    all_gather x1, waiting for transfers between devices, gather_weights(): return lax.all_gather(block, ('z', 'c'), axis=0, tiled=True)  8.58 us
    pallas_call x1, Pallas kernels, spatial(): pl.pallas_call(functools.partial(spatial_kernel, group), out_shape=jax.Sh...  4.9 us
  transfers between devices with their start and end apart: 2, of which 2 were waited for; matrix products, arithmetic and copies ran while one was open for 1% of the time, Pallas kernels for 3%

profile of v1, /device:TPU:1, one launch (start us, length us, event | category | flops | bytes accessed | tf_op | source)
XLA Modules:
  0.0 178.2 jit_solution(3143459438560382603)
XLA Ops:
  6.5 0.8 reshape.54
  7.4 0.1 fusion.2
  7.5 1.0 broadcast_in_dim.21
  8.5 10.4 %all-to-all-start.2 = ((bf16[32,2,24,192]{3,2,1,0:T(8,128)(2,1)}), bf16[32,2,24,192]{3,2,1,0:T(8,128)(2,1)S(1)}, u32[]{:S(2)}, u32[]{:S(2)}) async-start(bf16[32,2,24,192]{3,2,1,0:T(8,128)(2,1)} %bitcast.2), calls=%async_computation.2 | async-start | bytes 1572864 | tf_op jit(solution)/shard_map/all_to_all | solution.py:107
  19.0 0.0 all-gather.2.cloned.1.call-start
  19.1 14.3 %all-to-all-done.2 = bf16[32,2,24,192]{3,2,1,0:T(8,128)(2,1)S(1)} async-done(((bf16[32,2,24,192]{3,2,1,0:T(8,128)(2,1)}), bf16[32,2,24,192]{3,2,1,0:T(8,128)(2,1)S(1)}, u32[]{:S(2)}, u32[]{:S(2)}) %all-to-all-start.2) | async-done | bytes 589856 | tf_op jit(solution)/shard_map/all_to_all | solution.py:107
  33.6 0.8 concatenate.28
  34.3 0.0 all-gather.2.cloned.1.call-update
  35.0 4.9 %spatial.1 = bf16[128,1536]{1,0:T(8,128)(2,1)} custom-call(s32[1]{0:T(128)S(6)} %copy.16.idx_ref, bf16[1,1,128,1536]{3,2,1,0:T(8,128)(2,1)} %q_ref.1, bf16[1,1,128,1536]{3,2,1,0:T(8,128)(2,1)} %k_ref.1, bf16[1,1,128,1536]{3,2,1,0:T(8,128)(2,1)} %v_ref.1, f32[64,2,1536]{2,1,0:T(2,128)} %ada_ref.1), custom_call_target="tpu_custom_call" | custom-call | flops 100663296 | bytes 1572864 | tf_op jit(solution)/shard_map/spatial/pallas_call | solution.py:50
  39.9 1.1 reshape.53
  41.1 44.6 %all_to_all.20 = bf16[64,2,1536]{2,1,0:T(2,128)(2,1)S(1)} all-to-all(bf16[64,2,1536]{2,1,0:T(2,128)(2,1)S(1)} %reshape.53), channel_id=1, replica_groups=mesh['z'=16,'xl'=2,'c'=2,'y'=4,'xh'=2] {'z','xl','c'}, dimensions={0} | all-to-all | bytes 786432 | tf_op jit(solution)/shard_map/all_to_all | solution.py:124
  85.7 0.1 broadcast_in_dim.17
  85.9 0.1 broadcast_in_dim.18
  86.0 22.3 %all_to_all.21.x_ref = bf16[4,128,1536]{2,1,0:T(8,128)(2,1)} all-to-all(bf16[4,128,1536]{2,1,0:T(8,128)(2,1)S(1)} %broadcast_in_dim.18), channel_id=1, replica_groups=mesh['z'=16,'xl'=2,'c'=2,'y'=4,'xh'=2] {'y'}, dimensions={0} | all-to-all | bytes 3145728 | tf_op jit(solution)/shard_map/all_to_all | solution.py:126
  108.3 8.6 %all-gather.2.cloned.1.call-done.w_ref = bf16[1536,1152]{1,0:T(8,128)(2,1)} async-done(((bf16[48,1152]{1,0:T(8,128)(2,1)}), bf16[1536,1152]{1,0:T(8,128)(2,1)}) %all-gather.2.cloned.1.call-update) | async-done | bytes 3538960 | tf_op jit(solution)/shard_map/all_gather | solution.py:117
  116.9 9.2 %temporal.1 = bf16[4,128,384]{2,1,0:T(8,128)(2,1)} custom-call(bf16[4,128,1536]{2,1,0:T(8,128)(2,1)} %all_to_all.21.x_ref, bf16[1536,1152]{1,0:T(8,128)(2,1)} %all-gather.2.cloned.1.call-done.w_ref), custom_call_target="tpu_custom_call" | custom-call | flops 1811939328 | bytes 6291456 | tf_op jit(solution)/shard_map/temporal/pallas_call | solution.py:82
  126.1 1.1 reshape.57
  127.2 0.3 copy.14
  127.5 42.8 %all_to_all.22 = bf16[256,2,384]{2,1,0:T(2,128)(2,1)S(1)} all-to-all(bf16[256,2,384]{2,1,0:T(2,128)(2,1)S(1)} %bitcast.19), channel_id=1, replica_groups=mesh['z'=16,'xl'=2,'c'=2,'y'=4,'xh'=2] {'z','xl','c','y'}, dimensions={0} | all-to-all | bytes 786432 | tf_op jit(solution)/shard_map/all_to_all | solution.py:129
  170.3 0.2 copy.15
  170.4 0.9 reshape.60
  (5 shorter events, 0.1 us)
Async XLA Ops:
  8.5 25.0 %all-to-all-start.2 = ((bf16[32,2,24,192]{3,2,1,0:T(8,128)(2,1)}), bf16[32,2,24,192]{3,2,1,0:T(8,128)(2,1)S(1)}, u32[]{:S(2)}, u32[]{:S(2)}) async-start(bf16[32,2,24,192]{3,2,1,0:T(8,128)(2,1)} %bitcast.2), calls=%async_computation.2 | async-start | bytes 1572864 | tf_op jit(solution)/shard_map/all_to_all | solution.py:107
  19.0 97.9 %all-gather.2.cloned.1.call-start = ((), (), s32[]{:S(2)}) async-start(), calls=%async_computation.4 | async-start | bytes 3649536 | tf_op jit(solution)/shard_map/all_gather | solution.py:117
Sparse Core Ops, SparseCore 0:
  34.5 82.3 all-gather.1

commit v2 on v1

v2 whole, which is shorter than its diff:
```python
import functools
import jax
import jax.numpy as jnp
from jax import lax
from jax.experimental import pallas as pl
from jax.experimental.pallas import tpu as pltpu
from jax.sharding import Mesh, PartitionSpec as P
HEADS=12; HEAD_SIZE=128; ITERS=3; POWER=0.8; EPS=1e-6


def transport(scores):
    col = None
    for _ in range(ITERS):
        shifted = scores if col is None else scores + col
        top = jnp.max(shifted, axis=-1, keepdims=True)
        row = -POWER * (top + jnp.log(jnp.sum(jnp.exp(shifted - top), axis=-1, keepdims=True)))
        shifted = scores + row
        top = jnp.max(shifted, axis=-2, keepdims=True)
        col = -POWER * (top + jnp.log(jnp.sum(jnp.exp(shifted - top), axis=-2, keepdims=True)))
    return jnp.exp(shifted + col).astype(jnp.bfloat16)


def spatial_kernel(group, idx_ref, q_ref, k_ref, v_ref, ada_ref, o_ref, acc_ref):
    step = pl.program_id(0)
    scale = 1.0 / HEAD_SIZE**0.5
    scores = []
    for h in range(group):
        lanes = slice(h*HEAD_SIZE,(h+1)*HEAD_SIZE)
        scores.append(lax.dot_general(q_ref[0,0,:,lanes], k_ref[0,0,:,lanes], (((1,),(1,)),((),())), preferred_element_type=jnp.float32)*scale)
    plan = transport(jnp.stack(scores))
    for h in range(group):
        lanes = slice(h*HEAD_SIZE,(h+1)*HEAD_SIZE)
        out = jnp.dot(plan[h], v_ref[0,0,:,lanes], preferred_element_type=jnp.float32).astype(jnp.bfloat16)
        acc_ref[step, :, lanes] = out

    @pl.when(step == pl.num_programs(0)-1)
    def _():
        n = HEADS//group
        total = None
        for s in range(n):
            part = acc_ref[s].astype(jnp.float32)
            part = jnp.sum(part*part, axis=-1, keepdims=True)
            total = part if total is None else total + part
        inv = lax.rsqrt(total/(HEADS*HEAD_SIZE) + EPS)
        w = group*HEAD_SIZE
        for s in range(n):
            part = acc_ref[s].astype(jnp.float32)
            o_ref[:, s*w:(s+1)*w] = (part*inv*(1.0+ada_ref[0,0:1,s*w:(s+1)*w])+ada_ref[0,1:2,s*w:(s+1)*w]).astype(jnp.bfloat16)


def spatial(idx, q, k, v, ada, group=3):
    width=HEADS*HEAD_SIZE; pos=q.shape[2]
    blk = pl.BlockSpec((1,1,pos,group*HEAD_SIZE), lambda i, idx: (0,0,0,i))
    return pl.pallas_call(
        functools.partial(spatial_kernel, group),
        out_shape=jax.ShapeDtypeStruct((pos,width), jnp.bfloat16),
        grid_spec=pltpu.PrefetchScalarGridSpec(
            num_scalar_prefetch=1, grid=(HEADS//group,),
            in_specs=[blk,blk,blk,pl.BlockSpec((1,2,width), lambda i, idx: (idx[0],0,0))],
            out_specs=pl.BlockSpec((pos,width), lambda i, idx: (0,0)),
            scratch_shapes=[pltpu.VMEM((HEADS//group,pos,group*HEAD_SIZE), jnp.bfloat16)]),
        compiler_params=pltpu.CompilerParams(dimension_semantics=("arbitrary",)),
        cost_estimate=pl.CostEstimate(flops=2*2*12*128*128*128, transcendentals=12*7*128*128, bytes_accessed=4*128*1536*2),
        name="spatial",
    )(idx, q, k, v, ada)


def temporal_kernel(positions, here_ref, x_ref, *refs):
    blocks, o_ref, w_ref, sem = refs[:8], refs[8], refs[9], refs[10]
    x_here, c_here = here_ref[0], here_ref[1]

    def copy(i):
        far = lax.rem(x_here + 4 - i // 2, 4)
        core = lax.rem(c_here + i % 2, 2)
        return pltpu.make_async_copy(blocks[i], w_ref.at[lax.div(far, 2), :, lax.rem(far, 2), core], sem.at[i])

    @pl.when(pl.program_id(0) == 0)
    def _():
        for i in range(8):
            copy(i).start()
        for i in range(8):
            copy(i).wait()

    scale = 1.0 / HEAD_SIZE**0.5
    vids, n, width = o_ref.shape[0], x_ref.shape[1], x_ref.shape[2]
    x = x_ref[pl.ds(pl.program_id(0) * vids, vids)].reshape(vids * n, width)
    whole = w_ref.reshape(2, width, w_ref.shape[-1])
    part = [jnp.dot(x, whole[e], preferred_element_type=jnp.float32).astype(jnp.bfloat16) for e in range(2)]
    full, half = HEAD_SIZE, HEAD_SIZE // 2
    triple = []
    for j in range(3):
        first = part[0][:, j * full:(j + 1) * full]
        last = part[1][:, j * full:(j + 1) * full]
        cut = slice(3 * full + j * half, 3 * full + (j + 1) * half)
        middle = jnp.concatenate([part[0][:, cut], part[1][:, cut]], axis=-1)
        triple.append((first, middle, last))
    same = (lax.broadcasted_iota(jnp.int32, (n, n), 0) % positions) == (lax.broadcasted_iota(jnp.int32, (n, n), 1) % positions)
    scores = []
    for b in range(vids):
        for h in range(3):
            rows = slice(b * n, (b + 1) * n)
            s = lax.dot_general(triple[0][h][rows], triple[1][h][rows], (((1,), (1,)), ((), ())), preferred_element_type=jnp.float32) * scale
            scores.append(jnp.where(same, s, -1e30))
    plan = transport(jnp.stack(scores))
    for b in range(vids):
        for h in range(3):
            rows = slice(b * n, (b + 1) * n)
            o_ref[b, :, h * full:(h + 1) * full] = jnp.dot(plan[b * 3 + h], triple[2][h][rows], preferred_element_type=jnp.float32).astype(jnp.bfloat16)


def temporal(here, x, blocks, positions, group):
    vids, n, width = x.shape
    cols = 3 * HEAD_SIZE
    z, rows, piece = blocks[0].shape
    return pl.pallas_call(
        functools.partial(temporal_kernel, positions),
        out_shape=jax.ShapeDtypeStruct((vids, n, cols), jnp.bfloat16),
        grid_spec=pltpu.PrefetchScalarGridSpec(
            num_scalar_prefetch=1,
            grid=(vids // group,),
            in_specs=[pl.BlockSpec(memory_space=pltpu.VMEM)] + [pl.BlockSpec(memory_space=pltpu.HBM)] * 8,
            out_specs=pl.BlockSpec((group, n, cols), lambda i, here: (i, 0, 0)),
            scratch_shapes=[pltpu.VMEM((2, z, 2, 2, rows, piece), jnp.bfloat16), pltpu.SemaphoreType.DMA((8,))]),
        compiler_params=pltpu.CompilerParams(dimension_semantics=("arbitrary",), vmem_limit_bytes=50 * 1024 * 1024),
        cost_estimate=pl.CostEstimate(flops=2 * vids * n * width * 3 * cols, transcendentals=vids * 3 * 7 * n * n, bytes_accessed=6 * 1024 * 1024),
        name="temporal",
    )(here, x, *blocks)


UNIT = 192
PIECES = 3
RING = (0, 2, 1, 3)


def everyone(x, axes, count):
    return lax.all_to_all(jnp.broadcast_to(x[None], (count,) + x.shape), axes, split_axis=0, concat_axis=0, tiled=True)


def gather_weights(w):
    rows = w.shape[0]
    me = lax.axis_index("y") * 2 + lax.axis_index("xh")
    found = []
    for i in range(PIECES):
        found.append(lax.ppermute(w[:, i * UNIT:(i + 1) * UNIT], ("y", "xh"), [(g, (PIECES * g + i) % 8) for g in range(8)]))
    found = jnp.stack(found)
    parts = [lax.dynamic_index_in_dim(found, (me + 8 * part) % PIECES, 0, keepdims=False) for part in range(3)]
    low = lax.axis_index("xh") == 0
    long = [jnp.where(low, p[:, :128], p[:, 64:]) for p in parts]
    short = [jnp.where(low, p[:, 128:], p[:, :64]) for p in parts]
    block = jnp.concatenate(long + short, axis=-1)
    block = lax.all_gather(block, "z", axis=0, tiled=True).reshape(16, rows, 3 * UNIT)
    return block


def spread(block):
    blocks = []
    for shift in range(4):
        near = lax.ppermute(block, ("xl", "xh"), [(RING.index(i), RING.index((i + shift) % 4)) for i in range(4)]) if shift else block
        blocks += [near, lax.ppermute(near, "c", [(0, 1), (1, 0)])]
    return blocks


def local(q_s, k_s, v_s, time_index, ada_table, w_temporal):
    width = HEADS * HEAD_SIZE
    here = jnp.stack([lax.axis_index("xh") * 2 + lax.axis_index("xl"), lax.axis_index("c")])
    weights = spread(gather_weights(w_temporal))
    modulated = spatial(time_index, q_s, k_s, v_s, ada_table, 6)
    modulated, here = lax.optimization_barrier((modulated, here))
    relayed = lax.all_to_all(modulated.reshape(64, 2, width), ("z", "xl", "c"), split_axis=0, concat_axis=0, tiled=True)
    tokens = everyone(relayed.reshape(128, width), "y", 4)
    out = temporal(here, tokens, weights, 2, 2)
    out = out.reshape(4, 64, 2, 384).transpose(1, 0, 2, 3).reshape(256, 2, 384)
    out = lax.all_to_all(out, ("z", "xl", "c", "y"), split_axis=0, concat_axis=0, tiled=True)
    out = out.reshape(64, 4, 2, 384).transpose(0, 2, 1, 3)
    return out.reshape(1, 1, 128, width)


def solution(mesh):
    fine = Mesh(mesh.devices.reshape(16, 2, 2, 4, 2), ("z", "xl", "c", "y", "xh"))
    seq, fsdp = ("z", "xl", "c"), ("y", "xh")
    frames = P(fsdp, seq, None, None)
    in_specs = (frames, frames, frames, P(fsdp), P(), P(seq, fsdp))
    return jax.shard_map(local, mesh=fine, in_specs=in_specs, out_specs=frames, check_vma=False)
```

time: 179 us -> 171 us (0.955)
  starting transfers between devices: 10.5 us -> 65.7 us
  blocking collectives: 110 us -> 64.2 us
  between operations: 14.2 us -> 0.96 us
  waiting for transfers between devices: 22.9 us -> 18.4 us
    all_to_all x2 -> x0, blocking collectives: 66.9 us -> none  [the longest x1 44.6 us: local(): lax.all_to_all(modulated.reshape(64, 2, width), ('z', 'xl', 'c'), split_a...]
    ppermute x0 -> x10, starting transfers between devices: none -> 43.3 us  [the longest x4 23.2 us: spread(): blocks += [near, lax.ppermute(near, 'c', [(0, 1), (1, 0)])]]
    all_gather x0 -> x1, blocking collectives: none -> 24.3 us  [gather_weights(): lax.all_gather(block, 'z', axis=0, tiled=True).reshape(16, rows, 3 * UNIT)]
    all_to_all x1 -> x2, starting transfers between devices: 10.4 us -> 22.4 us  [the longest x1 18.1 us: local(): lax.all_to_all(modulated.reshape(64, 2, width), ('z', 'xl', 'c'), split_a...]
    all_gather x1 -> x0, waiting for transfers between devices: 8.58 us -> none  [gather_weights(): return lax.all_gather(block, ('z', 'c'), axis=0, tiled=True)]
    all_to_all x1, blocking collectives: 42.8 us -> 40 us  [local(): lax.all_to_all(out, ('z', 'xl', 'c', 'y'), split_axis=0, concat_axis=0, t...]
    ppermute x0 -> x10, waiting for transfers between devices: none -> 2.74 us  [the longest x3 1.96 us: gather_weights(): lax.ppermute(w[:, i * UNIT:(i + 1) * UNIT], ('y', 'xh'), [(g, (PIECES * g...]
    unnamed x0 -> x6, local copies, waits for them, and re-layouts: none -> 1.82 us
  transfers between devices with their start and end apart: 2 -> 12, of which waited for: 2 -> 3; matrix products, arithmetic and copies ran while one was open for 1% -> 0% of each run, Pallas kernels for 3% -> 0%
where the time goes in v2:
time: 171 us; the launch traced here: 170 us
  starting transfers between devices  65.7 us (38%)
  blocking collectives  64.2 us (38%)
  waiting for transfers between devices  18.4 us (11%)
  Pallas kernels  13.6 us (8%)
  local copies, waits for them, and re-layouts  6.78 us (4%)
    all_to_all x1, blocking collectives, local(): lax.all_to_all(out, ('z', 'xl', 'c', 'y'), split_axis=0, concat_axis=0, t...  40 us
    all_gather x1, blocking collectives, gather_weights(): lax.all_gather(block, 'z', axis=0, tiled=True).reshape(16, rows, 3 * UNIT)  24.3 us
    ppermute x4, starting transfers between devices, spread(): blocks += [near, lax.ppermute(near, 'c', [(0, 1), (1, 0)])]  23.2 us
    all_to_all x1, starting transfers between devices, local(): lax.all_to_all(modulated.reshape(64, 2, width), ('z', 'xl', 'c'), split_a...  18.1 us
    all_to_all x1, waiting for transfers between devices, local(): lax.all_to_all(modulated.reshape(64, 2, width), ('z', 'xl', 'c'), split_a...  15.7 us
    ppermute x3, starting transfers between devices, spread(): lax.ppermute(block, ('xl', 'xh'), [(RING.index(i), RING.index((i + shift)...  10.2 us
    ppermute x3, starting transfers between devices, gather_weights(): lax.ppermute(w[:, i * UNIT:(i + 1) * UNIT], ('y', 'xh'), [(g, (PIECES * g...  9.83 us
    pallas_call x1, Pallas kernels, temporal(): pl.pallas_call(functools.partial(temporal_kernel, positions), out_shape=j...  8.67 us
  transfers between devices with their start and end apart: 12, of which 3 were waited for; matrix products, arithmetic and copies ran while one was open for 0% of the time, Pallas kernels for 0%

profile of v2, /device:TPU:1, one launch (start us, length us, event | category | flops | bytes accessed | tf_op | source)
XLA Modules:
  0.0 169.9 jit_solution(3963561995114680323)
XLA Ops:
  0.7 0.1 pad_add_fusion.here_ref
  0.7 0.0 copy-start.2
  0.7 4.9 %spatial.1 = bf16[128,1536]{1,0:T(8,128)(2,1)} custom-call(s32[1]{0:T(128)S(6)} %copy.10.idx_ref, bf16[1,1,128,1536]{3,2,1,0:T(8,128)(2,1)} %q_ref.1, bf16[1,1,128,1536]{3,2,1,0:T(8,128)(2,1)} %k_ref.1, bf16[1,1,128,1536]{3,2,1,0:T(8,128)(2,1)} %v_ref.1, f32[64,2,1536]{2,1,0:T(2,128)} %ada_ref.1), custom_call_target="tpu_custom_call" | custom-call | flops 100663296 | bytes 1572864 | tf_op jit(solution)/shard_map/spatial/pallas_call | solution.py:54
  5.6 1.9 %reshape.19 = bf16[64,2,1536]{2,1,0:T(2,128)(2,1)} reshape(bf16[128,1536]{1,0:T(8,128)(2,1)} %spatial.1) | data formatting | bytes 786432 | tf_op jit(solution)/shard_map/reshape | solution.py:169
  7.5 18.1 %all-to-all-start = ((bf16[64,2,1536]{2,1,0:T(2,128)(2,1)}), bf16[64,2,1536]{2,1,0:T(2,128)(2,1)S(1)}, u32[]{:S(2)}, u32[]{:S(2)}) async-start(bf16[64,2,1536]{2,1,0:T(2,128)(2,1)} %reshape.19), calls=%async_computation | async-start | bytes 786432 | tf_op jit(solution)/shard_map/all_to_all | solution.py:169
  25.6 0.0 copy-done.2
  25.6 0.1 fusion
  25.7 3.2 %collective-permute-start.2 = (bf16[24,192]{1,0:T(8,128)(2,1)S(1)}, bf16[24,192]{1,0:T(8,128)(2,1)S(1)}, u32[]{:S(2)}, u32[]{:S(2)}) collective-permute-start(bf16[24,192]{1,0:T(8,128)(2,1)S(1)} %get-tuple-element.13), channel_id=1, source_target_pairs={{0,2},{1,5},{2,0},{3,3},{4,6},{5,1},{6,4},{7,7},{8,10},{9,13},{10,... | collective-permute-start | bytes 27656 | tf_op jit(solution)/shard_map/ppermute | solution.py:144
  28.9 6.0 %collective-permute-start.1 = (bf16[24,192]{1,0:T(8,128)(2,1)S(1)}, bf16[24,192]{1,0:T(8,128)(2,1)S(1)}, u32[]{:S(2)}, u32[]{:S(2)}) collective-permute-start(bf16[24,192]{1,0:T(8,128)(2,1)S(1)} %get-tuple-element.14), channel_id=1, source_target_pairs={{0,1},{1,4},{2,7},{3,2},{4,5},{5,0},{6,3},{7,6},{8,9},{9,12},{10,1... | collective-permute-start | bytes 27656 | tf_op jit(solution)/shard_map/ppermute | solution.py:144
  34.9 0.7 collective-permute-start
  35.6 0.0 collective-permute-done.2
  35.6 2.0 %collective-permute-done.1 = bf16[24,192]{1,0:T(8,128)(2,1)S(1)} collective-permute-done((bf16[24,192]{1,0:T(8,128)(2,1)S(1)}, bf16[24,192]{1,0:T(8,128)(2,1)S(1)}, u32[]{:S(2)}, u32[]{:S(2)}) %collective-permute-start.1) | collective-permute-done | bytes 9248 | tf_op jit(solution)/shard_map/ppermute | solution.py:144
  37.6 0.0 collective-permute-done
  37.6 0.1 slice_select_fusion.5
  37.7 0.1 slice_select_fusion.3
  37.8 15.7 %all-to-all-done = bf16[64,2,1536]{2,1,0:T(2,128)(2,1)S(1)} async-done(((bf16[64,2,1536]{2,1,0:T(2,128)(2,1)}), bf16[64,2,1536]{2,1,0:T(2,128)(2,1)S(1)}, u32[]{:S(2)}, u32[]{:S(2)}) %all-to-all-start) | async-done | bytes 393248 | tf_op jit(solution)/shard_map/all_to_all | solution.py:169
  53.4 0.1 broadcast_in_dim.7
  53.6 1.3 broadcast_in_dim.8
  54.9 4.3 %all-to-all-start.1 = ((bf16[4,128,1536]{2,1,0:T(8,128)(2,1)}), bf16[4,128,1536]{2,1,0:T(8,128)(2,1)}, u32[]{:S(2)}, u32[]{:S(2)}) async-start(bf16[4,128,1536]{2,1,0:T(8,128)(2,1)} %broadcast_in_dim.8), calls=%async_computation.1 | async-start | bytes 3145728 | tf_op jit(solution)/shard_map/all_to_all | solution.py:136
  59.2 0.1 concatenate.3
  59.3 24.3 %all_gather.3 = bf16[384,576]{1,0:T(8,128)(2,1)S(1)} all-gather(bf16[24,576]{1,0:T(8,128)(2,1)S(1)} %concatenate.3), channel_id=1, replica_groups=mesh['z'=16,'xl'=2,'c'=2,'y'=4,'xh'=2] {'z'}, dimensions={0}, use_global_device_ids=true | all-gather | bytes 470016 | tf_op jit(solution)/shard_map/all_gather | solution.py:151
  83.6 1.9 %collective-permute-start.4 = (bf16[16,24,576]{2,1,0:T(8,128)(2,1)S(1)}, bf16[16,24,576]{2,1,0:T(8,128)(2,1)S(1)}, u32[]{:S(2)}, u32[]{:S(2)}) collective-permute-start(bf16[16,24,576]{2,1,0:T(8,128)(2,1)S(1)} %bitcast.18), channel_id=1, source_target_pairs={{0,16},{16,1},{1,17},{17,0},{2,18},{18,3},{3,19},{19,2},{4,20},{20... | collective-permute-start | bytes 1327112 | tf_op jit(solution)/shard_map/ppermute | solution.py:158
  85.5 4.4 %collective-permute-start.6 = (bf16[16,24,576]{2,1,0:T(8,128)(2,1)S(1)}, bf16[16,24,576]{2,1,0:T(8,128)(2,1)S(1)}, u32[]{:S(2)}, u32[]{:S(2)}) collective-permute-start(bf16[16,24,576]{2,1,0:T(8,128)(2,1)S(1)} %bitcast.19), channel_id=1, source_target_pairs={{0,1},{16,17},{1,0},{17,16},{2,3},{18,19},{3,2},{19,18},{4,5},{20,... | collective-permute-start | bytes 1327112 | tf_op jit(solution)/shard_map/ppermute | solution.py:158
  89.9 4.0 %collective-permute-start.8 = (bf16[16,24,576]{2,1,0:T(8,128)(2,1)S(1)}, bf16[16,24,576]{2,1,0:T(8,128)(2,1)S(1)}, u32[]{:S(2)}, u32[]{:S(2)}) collective-permute-start(bf16[16,24,576]{2,1,0:T(8,128)(2,1)S(1)} %bitcast.20), channel_id=1, source_target_pairs={{0,17},{16,0},{1,16},{17,1},{2,19},{18,2},{3,18},{19,3},{4,21},{20... | collective-permute-start | bytes 1327112 | tf_op jit(solution)/shard_map/ppermute | solution.py:158
  93.9 8.3 %collective-permute-start.3 = (bf16[16,24,576]{2,1,0:T(8,128)(2,1)S(1)}, bf16[16,24,576]{2,1,0:T(8,128)(2,1)S(1)}, u32[]{:S(2)}, u32[]{:S(2)}) collective-permute-start(bf16[16,24,576]{2,1,0:T(8,128)(2,1)S(1)} %bitcast.21), channel_id=1, source_target_pairs={{0,8},{8,0},{1,9},{9,1},{2,10},{10,2},{3,11},{11,3},{4,12},{12,4},... | collective-permute-start | bytes 1327112 | tf_op jit(solution)/shard_map/ppermute | solution.py:159
  102.2 0.0 collective-permute-done.4.refs_2_
  102.2 10.6 %collective-permute-start.5 = (bf16[16,24,576]{2,1,0:T(8,128)(2,1)S(1)}, bf16[16,24,576]{2,1,0:T(8,128)(2,1)S(1)}, u32[]{:S(2)}, u32[]{:S(2)}) collective-permute-start(bf16[16,24,576]{2,1,0:T(8,128)(2,1)S(1)} %collective-permute-done.4.refs_2_), channel_id=1, source_target_pairs={{0,8},{8,0},{1,9},{9,1},{2,10},{10,2},{3,11},{11,3},{4,12},{12,4},... | collective-permute-start | bytes 1327112 | tf_op jit(solution)/shard_map/ppermute | solution.py:159
  112.8 0.0 collective-permute-done.6.refs_4_
  112.8 1.9 %collective-permute-start.7 = (bf16[16,24,576]{2,1,0:T(8,128)(2,1)S(1)}, bf16[16,24,576]{2,1,0:T(8,128)(2,1)S(1)}, u32[]{:S(2)}, u32[]{:S(2)}) collective-permute-start(bf16[16,24,576]{2,1,0:T(8,128)(2,1)S(1)} %collective-permute-done.6.refs_4_), channel_id=1, source_target_pairs={{0,8},{8,0},{1,9},{9,1},{2,10},{10,2},{3,11},{11,3},{4,12},{12,4},... | collective-permute-start | bytes 1327112 | tf_op jit(solution)/shard_map/ppermute | solution.py:159
  114.7 0.0 collective-permute-done.8.refs_6_
  114.7 2.4 %collective-permute-start.9 = (bf16[16,24,576]{2,1,0:T(8,128)(2,1)S(1)}, bf16[16,24,576]{2,1,0:T(8,128)(2,1)}, u32[]{:S(2)}, u32[]{:S(2)}) collective-permute-start(bf16[16,24,576]{2,1,0:T(8,128)(2,1)S(1)} %collective-permute-done.8.refs_6_), channel_id=1, source_target_pairs={{0,8},{8,0},{1,9},{9,1},{2,10},{10,2},{3,11},{11,3},{4,12},{12,4},... | collective-permute-start | bytes 1327112 | tf_op jit(solution)/shard_map/ppermute | solution.py:159
  117.2 0.0 collective-permute-done.3.refs_1_
  117.2 0.0 collective-permute-done.5.refs_3_
  117.2 0.0 collective-permute-done.7.refs_5_
  117.2 0.0 copy-start
  117.2 0.8 copy-done
  118.0 0.8 collective-permute-done.9.refs_7_
  118.8 0.0 all-to-all-done.1.x_ref
  118.8 0.0 copy-start.1
  118.8 1.0 copy-done.1
  119.8 8.7 %temporal.1 = bf16[4,128,384]{2,1,0:T(8,128)(2,1)S(1)} custom-call(s32[2]{0:T(128)S(1)} %pad_add_fusion.here_ref, bf16[4,128,1536]{2,1,0:T(8,128)(2,1)} %all-to-all-done.1.x_ref, bf16[16,24,576]{2,1,0:T(8,128)(2,1)S(1)} %bitcast.22, bf16[16,24,576]{2,1,0:T(8,128)(2,1)S(1)} %collective-permute-done.3.refs_1_, ...), custom_call_target="tpu_custom_call" | custom-call | flops 1811939328 | bytes 6291456 | tf_op jit(solution)/shard_map/temporal/pallas_call | solution.py:115
  128.5 0.1 reshape.21
  128.6 0.3 copy.8
  128.9 40.0 %all_to_all.15 = bf16[256,2,384]{2,1,0:T(2,128)(2,1)S(1)} all-to-all(bf16[256,2,384]{2,1,0:T(2,128)(2,1)S(1)} %bitcast.23), channel_id=1, replica_groups=mesh['z'=16,'xl'=2,'c'=2,'y'=4,'xh'=2] {'z','xl','c','y'}, dimensions={0} | all-to-all | bytes 786432 | tf_op jit(solution)/shard_map/all_to_all | solution.py:173
  168.9 0.2 copy.9
  169.0 0.9 reshape.24
  (4 shorter events, 0.0 us)
Async XLA Ops:
  0.7 24.9 %copy-start.2 = (bf16[24,576]{1,0:T(8,128)(2,1)S(1)}, bf16[24,576]{1,0:T(8,128)(2,1)}, u32[]{:S(2)}) copy-start(bf16[24,576]{1,0:T(8,128)(2,1)} %param.11) | copy-start | bytes 82948
  7.5 45.9 %all-to-all-start = ((bf16[64,2,1536]{2,1,0:T(2,128)(2,1)}), bf16[64,2,1536]{2,1,0:T(2,128)(2,1)S(1)}, u32[]{:S(2)}, u32[]{:S(2)}) async-start(bf16[64,2,1536]{2,1,0:T(2,128)(2,1)} %reshape.19), calls=%async_computation | async-start | bytes 786432 | tf_op jit(solution)/shard_map/all_to_all | solution.py:169
  25.7 9.9 %collective-permute-start.2 = (bf16[24,192]{1,0:T(8,128)(2,1)S(1)}, bf16[24,192]{1,0:T(8,128)(2,1)S(1)}, u32[]{:S(2)}, u32[]{:S(2)}) collective-permute-start(bf16[24,192]{1,0:T(8,128)(2,1)S(1)} %get-tuple-element.13), channel_id=1, source_target_pairs={{0,2},{1,5},{2,0},{3,3},{4,6},{5,1},{6,4},{7,7},{8,10},{9,13},{10,... | collective-permute-start | bytes 27656 | tf_op jit(solution)/shard_map/ppermute | solution.py:144
  28.9 8.7 %collective-permute-start.1 = (bf16[24,192]{1,0:T(8,128)(2,1)S(1)}, bf16[24,192]{1,0:T(8,128)(2,1)S(1)}, u32[]{:S(2)}, u32[]{:S(2)}) collective-permute-start(bf16[24,192]{1,0:T(8,128)(2,1)S(1)} %get-tuple-element.14), channel_id=1, source_target_pairs={{0,1},{1,4},{2,7},{3,2},{4,5},{5,0},{6,3},{7,6},{8,9},{9,12},{10,1... | collective-permute-start | bytes 27656 | tf_op jit(solution)/shard_map/ppermute | solution.py:144
  34.9 2.7 %collective-permute-start = (bf16[24,192]{1,0:T(8,128)(2,1)S(1)}, bf16[24,192]{1,0:T(8,128)(2,1)S(1)}, u32[]{:S(2)}, u32[]{:S(2)}) collective-permute-start(bf16[24,192]{1,0:T(8,128)(2,1)S(1)} %get-tuple-element.12), channel_id=1, source_target_pairs={{0,0},{1,3},{2,6},{3,1},{4,4},{5,7},{6,2},{7,5},{8,8},{9,11},{10,1... | collective-permute-start | bytes 27656 | tf_op jit(solution)/shard_map/ppermute | solution.py:144
  54.9 63.9 %all-to-all-start.1 = ((bf16[4,128,1536]{2,1,0:T(8,128)(2,1)}), bf16[4,128,1536]{2,1,0:T(8,128)(2,1)}, u32[]{:S(2)}, u32[]{:S(2)}) async-start(bf16[4,128,1536]{2,1,0:T(8,128)(2,1)} %broadcast_in_dim.8), calls=%async_computation.1 | async-start | bytes 3145728 | tf_op jit(solution)/shard_map/all_to_all | solution.py:136
  83.6 18.6 %collective-permute-start.4 = (bf16[16,24,576]{2,1,0:T(8,128)(2,1)S(1)}, bf16[16,24,576]{2,1,0:T(8,128)(2,1)S(1)}, u32[]{:S(2)}, u32[]{:S(2)}) collective-permute-start(bf16[16,24,576]{2,1,0:T(8,128)(2,1)S(1)} %bitcast.18), channel_id=1, source_target_pairs={{0,16},{16,1},{1,17},{17,0},{2,18},{18,3},{3,19},{19,2},{4,20},{20... | collective-permute-start | bytes 1327112 | tf_op jit(solution)/shard_map/ppermute | solution.py:158
  85.5 27.3 %collective-permute-start.6 = (bf16[16,24,576]{2,1,0:T(8,128)(2,1)S(1)}, bf16[16,24,576]{2,1,0:T(8,128)(2,1)S(1)}, u32[]{:S(2)}, u32[]{:S(2)}) collective-permute-start(bf16[16,24,576]{2,1,0:T(8,128)(2,1)S(1)} %bitcast.19), channel_id=1, source_target_pairs={{0,1},{16,17},{1,0},{17,16},{2,3},{18,19},{3,2},{19,18},{4,5},{20,... | collective-permute-start | bytes 1327112 | tf_op jit(solution)/shard_map/ppermute | solution.py:158
  89.9 24.8 %collective-permute-start.8 = (bf16[16,24,576]{2,1,0:T(8,128)(2,1)S(1)}, bf16[16,24,576]{2,1,0:T(8,128)(2,1)S(1)}, u32[]{:S(2)}, u32[]{:S(2)}) collective-permute-start(bf16[16,24,576]{2,1,0:T(8,128)(2,1)S(1)} %bitcast.20), channel_id=1, source_target_pairs={{0,17},{16,0},{1,16},{17,1},{2,19},{18,2},{3,18},{19,3},{4,21},{20... | collective-permute-start | bytes 1327112 | tf_op jit(solution)/shard_map/ppermute | solution.py:158
  93.9 23.3 %collective-permute-start.3 = (bf16[16,24,576]{2,1,0:T(8,128)(2,1)S(1)}, bf16[16,24,576]{2,1,0:T(8,128)(2,1)S(1)}, u32[]{:S(2)}, u32[]{:S(2)}) collective-permute-start(bf16[16,24,576]{2,1,0:T(8,128)(2,1)S(1)} %bitcast.21), channel_id=1, source_target_pairs={{0,8},{8,0},{1,9},{9,1},{2,10},{10,2},{3,11},{11,3},{4,12},{12,4},... | collective-permute-start | bytes 1327112 | tf_op jit(solution)/shard_map/ppermute | solution.py:159
  102.2 14.9 %collective-permute-start.5 = (bf16[16,24,576]{2,1,0:T(8,128)(2,1)S(1)}, bf16[16,24,576]{2,1,0:T(8,128)(2,1)S(1)}, u32[]{:S(2)}, u32[]{:S(2)}) collective-permute-start(bf16[16,24,576]{2,1,0:T(8,128)(2,1)S(1)} %collective-permute-done.4.refs_2_), channel_id=1, source_target_pairs={{0,8},{8,0},{1,9},{9,1},{2,10},{10,2},{3,11},{11,3},{4,12},{12,4},... | collective-permute-start | bytes 1327112 | tf_op jit(solution)/shard_map/ppermute | solution.py:159
  112.8 4.4 %collective-permute-start.7 = (bf16[16,24,576]{2,1,0:T(8,128)(2,1)S(1)}, bf16[16,24,576]{2,1,0:T(8,128)(2,1)S(1)}, u32[]{:S(2)}, u32[]{:S(2)}) collective-permute-start(bf16[16,24,576]{2,1,0:T(8,128)(2,1)S(1)} %collective-permute-done.6.refs_4_), channel_id=1, source_target_pairs={{0,8},{8,0},{1,9},{9,1},{2,10},{10,2},{3,11},{11,3},{4,12},{12,4},... | collective-permute-start | bytes 1327112 | tf_op jit(solution)/shard_map/ppermute | solution.py:159
  114.7 4.0 %collective-permute-start.9 = (bf16[16,24,576]{2,1,0:T(8,128)(2,1)S(1)}, bf16[16,24,576]{2,1,0:T(8,128)(2,1)}, u32[]{:S(2)}, u32[]{:S(2)}) collective-permute-start(bf16[16,24,576]{2,1,0:T(8,128)(2,1)S(1)} %collective-permute-done.8.refs_6_), channel_id=1, source_target_pairs={{0,8},{8,0},{1,9},{9,1},{2,10},{10,2},{3,11},{11,3},{4,12},{12,4},... | collective-permute-start | bytes 1327112 | tf_op jit(solution)/shard_map/ppermute | solution.py:159
  117.2 0.8 copy-start
  118.8 1.0 copy-start.1

commit v3 on v2

--- a/solution.py
+++ b/solution.py
@@ -45,7 +45,7 @@
         w = group*HEAD_SIZE
         for s in range(n):
             part = acc_ref[s].astype(jnp.float32)
-            o_ref[:, s*w:(s+1)*w] = (part*inv*(1.0+ada_ref[0,0:1,s*w:(s+1)*w])+ada_ref[0,1:2,s*w:(s+1)*w]).astype(jnp.bfloat16)
+            o_ref[:, :, s*w:(s+1)*w] = (part*inv*(1.0+ada_ref[0,0:1,s*w:(s+1)*w])+ada_ref[0,1:2,s*w:(s+1)*w]).astype(jnp.bfloat16).reshape(o_ref.shape[0], o_ref.shape[1], w)
 
 
 def spatial(idx, q, k, v, ada, group=3):
@@ -53,11 +53,11 @@
     blk = pl.BlockSpec((1,1,pos,group*HEAD_SIZE), lambda i, idx: (0,0,0,i))
     return pl.pallas_call(
         functools.partial(spatial_kernel, group),
-        out_shape=jax.ShapeDtypeStruct((pos,width), jnp.bfloat16),
+        out_shape=jax.ShapeDtypeStruct((pos//2,2,width), jnp.bfloat16),
         grid_spec=pltpu.PrefetchScalarGridSpec(
             num_scalar_prefetch=1, grid=(HEADS//group,),
             in_specs=[blk,blk,blk,pl.BlockSpec((1,2,width), lambda i, idx: (idx[0],0,0))],
-            out_specs=pl.BlockSpec((pos,width), lambda i, idx: (0,0)),
+            out_specs=pl.BlockSpec((pos//2,2,width), lambda i, idx: (0,0,0)),
             scratch_shapes=[pltpu.VMEM((HEADS//group,pos,group*HEAD_SIZE), jnp.bfloat16)]),
         compiler_params=pltpu.CompilerParams(dimension_semantics=("arbitrary",)),
         cost_estimate=pl.CostEstimate(flops=2*2*12*128*128*128, transcendentals=12*7*128*128, bytes_accessed=4*128*1536*2),
@@ -121,7 +121,7 @@
             in_specs=[pl.BlockSpec(memory_space=pltpu.VMEM)] + [pl.BlockSpec(memory_space=pltpu.HBM)] * 8,
             out_specs=pl.BlockSpec((group, n, cols), lambda i, here: (i, 0, 0)),
             scratch_shapes=[pltpu.VMEM((2, z, 2, 2, rows, piece), jnp.bfloat16), pltpu.SemaphoreType.DMA((8,))]),
-        compiler_params=pltpu.CompilerParams(dimension_semantics=("arbitrary",), vmem_limit_bytes=50 * 1024 * 1024),
+        compiler_params=pltpu.CompilerParams(dimension_semantics=("arbitrary",), vmem_limit_bytes=51 * 1024 * 1024),
         cost_estimate=pl.CostEstimate(flops=2 * vids * n * width * 3 * cols, transcendentals=vids * 3 * 7 * n * n, bytes_accessed=6 * 1024 * 1024),
         name="temporal",
     )(here, x, *blocks)
@@ -164,11 +164,11 @@
     width = HEADS * HEAD_SIZE
     here = jnp.stack([lax.axis_index("xh") * 2 + lax.axis_index("xl"), lax.axis_index("c")])
     weights = spread(gather_weights(w_temporal))
-    modulated = spatial(time_index, q_s, k_s, v_s, ada_table, 6)
+    modulated = spatial(time_index, q_s, k_s, v_s, ada_table, 12)
     modulated, here = lax.optimization_barrier((modulated, here))
     relayed = lax.all_to_all(modulated.reshape(64, 2, width), ("z", "xl", "c"), split_axis=0, concat_axis=0, tiled=True)
     tokens = everyone(relayed.reshape(128, width), "y", 4)
-    out = temporal(here, tokens, weights, 2, 2)
+    out = temporal(here, tokens, weights, 2, 4)
     out = out.reshape(4, 64, 2, 384).transpose(1, 0, 2, 3).reshape(256, 2, 384)
     out = lax.all_to_all(out, ("z", "xl", "c", "y"), split_axis=0, concat_axis=0, tiled=True)
     out = out.reshape(64, 4, 2, 384).transpose(0, 2, 1, 3)

time: 171 us -> 166 us (0.971)
  local copies, waits for them, and re-layouts: 6.78 us -> 3.85 us
    reshape x1 -> x0, local copies, waits for them, and re-layouts: 1.89 us -> none  [local(): modulated.reshape(64, 2, width)]
where the time goes in v3:
time: 166 us
  starting transfers between devices  65.7 us (40%)
  blocking collectives  64.2 us (39%)
  waiting for transfers between devices  18.4 us (11%)
  Pallas kernels  12.2 us (7%)
  local copies, waits for them, and re-layouts  3.85 us (2%)
    all_to_all x1, blocking collectives, local(): lax.all_to_all(out, ('z', 'xl', 'c', 'y'), split_axis=0, concat_axis=0, t...  40 us
    all_gather x1, blocking collectives, gather_weights(): lax.all_gather(block, 'z', axis=0, tiled=True).reshape(16, rows, 3 * UNIT)  24.3 us
    ppermute x4, starting transfers between devices, spread(): blocks += [near, lax.ppermute(near, 'c', [(0, 1), (1, 0)])]  23.2 us
    all_to_all x1, starting transfers between devices, local(): lax.all_to_all(modulated.reshape(64, 2, width), ('z', 'xl', 'c'), split_a...  18.1 us
    all_to_all x1, waiting for transfers between devices, local(): lax.all_to_all(modulated.reshape(64, 2, width), ('z', 'xl', 'c'), split_a...  15.7 us
    ppermute x3, starting transfers between devices, spread(): lax.ppermute(block, ('xl', 'xh'), [(RING.index(i), RING.index((i + shift)...  10.2 us
    ppermute x3, starting transfers between devices, gather_weights(): lax.ppermute(w[:, i * UNIT:(i + 1) * UNIT], ('y', 'xh'), [(g, (PIECES * g...  9.82 us
    pallas_call x1, Pallas kernels, temporal(): pl.pallas_call(functools.partial(temporal_kernel, positions), out_shape=j...  7.95 us
  transfers between devices with their start and end apart: 12, of which 3 were waited for; matrix products, arithmetic and copies ran while one was open for 0% of the time, Pallas kernels for 0%

profile of v3, /device:TPU:1, one launch (start us, length us, event | category | flops | bytes accessed | tf_op | source)
XLA Modules:
  0.0 165.7 jit_solution(1059594821908303246)
XLA Ops:
  0.7 0.1 pad_add_fusion.here_ref
  0.7 0.0 copy-start
  0.7 4.3 %spatial.1 = bf16[64,2,1536]{2,1,0:T(2,128)(2,1)} custom-call(s32[1]{0:T(128)S(6)} %copy.10.idx_ref, bf16[1,1,128,1536]{3,2,1,0:T(8,128)(2,1)} %q_ref.1, bf16[1,1,128,1536]{3,2,1,0:T(8,128)(2,1)} %k_ref.1, bf16[1,1,128,1536]{3,2,1,0:T(8,128)(2,1)} %v_ref.1, f32[64,2,1536]{2,1,0:T(2,128)} %ada_ref.1), custom_call_target="tpu_custom_call" | custom-call | flops 100663296 | bytes 1572864 | tf_op jit(solution)/shard_map/spatial/pallas_call | solution.py:54
  5.0 18.1 %all-to-all-start = ((bf16[64,2,1536]{2,1,0:T(2,128)(2,1)}), bf16[64,2,1536]{2,1,0:T(2,128)(2,1)S(1)}, u32[]{:S(2)}, u32[]{:S(2)}) async-start(bf16[64,2,1536]{2,1,0:T(2,128)(2,1)} %spatial.1), calls=%async_computation | async-start | bytes 786432 | tf_op jit(solution)/shard_map/all_to_all | solution.py:169
  23.1 0.0 copy-done
  23.1 0.1 fusion
  23.2 3.2 %collective-permute-start.2 = (bf16[24,192]{1,0:T(8,128)(2,1)S(1)}, bf16[24,192]{1,0:T(8,128)(2,1)S(1)}, u32[]{:S(2)}, u32[]{:S(2)}) collective-permute-start(bf16[24,192]{1,0:T(8,128)(2,1)S(1)} %get-tuple-element.13), channel_id=1, source_target_pairs={{0,2},{1,5},{2,0},{3,3},{4,6},{5,1},{6,4},{7,7},{8,10},{9,13},{10,... | collective-permute-start | bytes 27656 | tf_op jit(solution)/shard_map/ppermute | solution.py:144
  26.4 6.0 %collective-permute-start.1 = (bf16[24,192]{1,0:T(8,128)(2,1)S(1)}, bf16[24,192]{1,0:T(8,128)(2,1)S(1)}, u32[]{:S(2)}, u32[]{:S(2)}) collective-permute-start(bf16[24,192]{1,0:T(8,128)(2,1)S(1)} %get-tuple-element.14), channel_id=1, source_target_pairs={{0,1},{1,4},{2,7},{3,2},{4,5},{5,0},{6,3},{7,6},{8,9},{9,12},{10,1... | collective-permute-start | bytes 27656 | tf_op jit(solution)/shard_map/ppermute | solution.py:144
  32.4 0.7 collective-permute-start
  33.1 0.0 collective-permute-done.2
  33.1 1.9 %collective-permute-done.1 = bf16[24,192]{1,0:T(8,128)(2,1)S(1)} collective-permute-done((bf16[24,192]{1,0:T(8,128)(2,1)S(1)}, bf16[24,192]{1,0:T(8,128)(2,1)S(1)}, u32[]{:S(2)}, u32[]{:S(2)}) %collective-permute-start.1) | collective-permute-done | bytes 9248 | tf_op jit(solution)/shard_map/ppermute | solution.py:144
  35.0 0.0 collective-permute-done
  35.1 0.1 slice_select_fusion.5
  35.2 0.1 slice_select_fusion.3
  35.3 15.7 %all-to-all-done = bf16[64,2,1536]{2,1,0:T(2,128)(2,1)S(1)} async-done(((bf16[64,2,1536]{2,1,0:T(2,128)(2,1)}), bf16[64,2,1536]{2,1,0:T(2,128)(2,1)S(1)}, u32[]{:S(2)}, u32[]{:S(2)}) %all-to-all-start) | async-done | bytes 393248 | tf_op jit(solution)/shard_map/all_to_all | solution.py:169
  51.0 0.1 broadcast_in_dim.7
  51.1 1.3 broadcast_in_dim.8
  52.4 4.3 %all-to-all-start.1 = ((bf16[4,128,1536]{2,1,0:T(8,128)(2,1)}), bf16[4,128,1536]{2,1,0:T(8,128)(2,1)}, u32[]{:S(2)}, u32[]{:S(2)}) async-start(bf16[4,128,1536]{2,1,0:T(8,128)(2,1)} %broadcast_in_dim.8), calls=%async_computation.1 | async-start | bytes 3145728 | tf_op jit(solution)/shard_map/all_to_all | solution.py:136
  56.7 0.1 concatenate.3
  56.8 24.3 %all_gather.3 = bf16[384,576]{1,0:T(8,128)(2,1)S(1)} all-gather(bf16[24,576]{1,0:T(8,128)(2,1)S(1)} %concatenate.3), channel_id=1, replica_groups=mesh['z'=16,'xl'=2,'c'=2,'y'=4,'xh'=2] {'z'}, dimensions={0}, use_global_device_ids=true | all-gather | bytes 470016 | tf_op jit(solution)/shard_map/all_gather | solution.py:151
  81.1 1.9 %collective-permute-start.4 = (bf16[16,24,576]{2,1,0:T(8,128)(2,1)S(1)}, bf16[16,24,576]{2,1,0:T(8,128)(2,1)S(1)}, u32[]{:S(2)}, u32[]{:S(2)}) collective-permute-start(bf16[16,24,576]{2,1,0:T(8,128)(2,1)S(1)} %bitcast.18), channel_id=1, source_target_pairs={{0,16},{16,1},{1,17},{17,0},{2,18},{18,3},{3,19},{19,2},{4,20},{20... | collective-permute-start | bytes 1327112 | tf_op jit(solution)/shard_map/ppermute | solution.py:158
  83.0 4.4 %collective-permute-start.6 = (bf16[16,24,576]{2,1,0:T(8,128)(2,1)S(1)}, bf16[16,24,576]{2,1,0:T(8,128)(2,1)S(1)}, u32[]{:S(2)}, u32[]{:S(2)}) collective-permute-start(bf16[16,24,576]{2,1,0:T(8,128)(2,1)S(1)} %bitcast.19), channel_id=1, source_target_pairs={{0,1},{16,17},{1,0},{17,16},{2,3},{18,19},{3,2},{19,18},{4,5},{20,... | collective-permute-start | bytes 1327112 | tf_op jit(solution)/shard_map/ppermute | solution.py:158
  87.4 4.0 %collective-permute-start.8 = (bf16[16,24,576]{2,1,0:T(8,128)(2,1)S(1)}, bf16[16,24,576]{2,1,0:T(8,128)(2,1)S(1)}, u32[]{:S(2)}, u32[]{:S(2)}) collective-permute-start(bf16[16,24,576]{2,1,0:T(8,128)(2,1)S(1)} %bitcast.20), channel_id=1, source_target_pairs={{0,17},{16,0},{1,16},{17,1},{2,19},{18,2},{3,18},{19,3},{4,21},{20... | collective-permute-start | bytes 1327112 | tf_op jit(solution)/shard_map/ppermute | solution.py:158
  91.4 8.3 %collective-permute-start.3 = (bf16[16,24,576]{2,1,0:T(8,128)(2,1)S(1)}, bf16[16,24,576]{2,1,0:T(8,128)(2,1)S(1)}, u32[]{:S(2)}, u32[]{:S(2)}) collective-permute-start(bf16[16,24,576]{2,1,0:T(8,128)(2,1)S(1)} %bitcast.21), channel_id=1, source_target_pairs={{0,8},{8,0},{1,9},{9,1},{2,10},{10,2},{3,11},{11,3},{4,12},{12,4},... | collective-permute-start | bytes 1327112 | tf_op jit(solution)/shard_map/ppermute | solution.py:159
  99.7 0.0 collective-permute-done.4.refs_2_
  99.7 10.6 %collective-permute-start.5 = (bf16[16,24,576]{2,1,0:T(8,128)(2,1)S(1)}, bf16[16,24,576]{2,1,0:T(8,128)(2,1)S(1)}, u32[]{:S(2)}, u32[]{:S(2)}) collective-permute-start(bf16[16,24,576]{2,1,0:T(8,128)(2,1)S(1)} %collective-permute-done.4.refs_2_), channel_id=1, source_target_pairs={{0,8},{8,0},{1,9},{9,1},{2,10},{10,2},{3,11},{11,3},{4,12},{12,4},... | collective-permute-start | bytes 1327112 | tf_op jit(solution)/shard_map/ppermute | solution.py:159
  110.3 0.0 collective-permute-done.6.refs_4_
  110.3 1.9 %collective-permute-start.7 = (bf16[16,24,576]{2,1,0:T(8,128)(2,1)S(1)}, bf16[16,24,576]{2,1,0:T(8,128)(2,1)S(1)}, u32[]{:S(2)}, u32[]{:S(2)}) collective-permute-start(bf16[16,24,576]{2,1,0:T(8,128)(2,1)S(1)} %collective-permute-done.6.refs_4_), channel_id=1, source_target_pairs={{0,8},{8,0},{1,9},{9,1},{2,10},{10,2},{3,11},{11,3},{4,12},{12,4},... | collective-permute-start | bytes 1327112 | tf_op jit(solution)/shard_map/ppermute | solution.py:159
  112.2 0.0 collective-permute-done.8.refs_6_
  112.2 0.0 copy-start.1
  112.3 2.4 %collective-permute-start.9 = (bf16[16,24,576]{2,1,0:T(8,128)(2,1)S(1)}, bf16[16,24,576]{2,1,0:T(8,128)(2,1)}, u32[]{:S(2)}, u32[]{:S(2)}) collective-permute-start(bf16[16,24,576]{2,1,0:T(8,128)(2,1)S(1)} %collective-permute-done.8.refs_6_), channel_id=1, source_target_pairs={{0,8},{8,0},{1,9},{9,1},{2,10},{10,2},{3,11},{11,3},{4,12},{12,4},... | collective-permute-start | bytes 1327112 | tf_op jit(solution)/shard_map/ppermute | solution.py:159
  114.7 0.0 collective-permute-done.3.refs_1_
  114.7 0.0 collective-permute-done.5.refs_3_
  114.7 0.0 collective-permute-done.7.refs_5_
  114.7 0.0 copy-start.2
  114.7 0.8 copy-done.2
  115.5 0.8 collective-permute-done.9.refs_7_
  116.3 0.0 all-to-all-done.1.x_ref
  116.3 0.0 copy-done.1
  116.3 7.9 %temporal.1 = bf16[4,128,384]{2,1,0:T(8,128)(2,1)S(1)} custom-call(s32[2]{0:T(128)S(1)} %pad_add_fusion.here_ref, bf16[4,128,1536]{2,1,0:T(8,128)(2,1)} %all-to-all-done.1.x_ref, bf16[16,24,576]{2,1,0:T(8,128)(2,1)S(1)} %bitcast.22, bf16[16,24,576]{2,1,0:T(8,128)(2,1)S(1)} %collective-permute-done.3.refs_1_, ...), custom_call_target="tpu_custom_call" | custom-call | flops 1811939328 | bytes 6291456 | tf_op jit(solution)/shard_map/temporal/pallas_call | solution.py:115
  124.2 0.1 reshape.17
  124.4 0.3 copy.8
  124.7 40.0 %all_to_all.15 = bf16[256,2,384]{2,1,0:T(2,128)(2,1)S(1)} all-to-all(bf16[256,2,384]{2,1,0:T(2,128)(2,1)S(1)} %bitcast.23), channel_id=1, replica_groups=mesh['z'=16,'xl'=2,'c'=2,'y'=4,'xh'=2] {'z','xl','c','y'}, dimensions={0} | all-to-all | bytes 786432 | tf_op jit(solution)/shard_map/all_to_all | solution.py:173
  164.6 0.2 copy.9
  164.8 0.9 reshape.20
  (4 shorter events, 0.0 us)
Async XLA Ops:
  0.7 22.4 %copy-start = (bf16[24,576]{1,0:T(8,128)(2,1)S(1)}, bf16[24,576]{1,0:T(8,128)(2,1)}, u32[]{:S(2)}) copy-start(bf16[24,576]{1,0:T(8,128)(2,1)} %param.11) | copy-start | bytes 82948
  5.0 45.9 %all-to-all-start = ((bf16[64,2,1536]{2,1,0:T(2,128)(2,1)}), bf16[64,2,1536]{2,1,0:T(2,128)(2,1)S(1)}, u32[]{:S(2)}, u32[]{:S(2)}) async-start(bf16[64,2,1536]{2,1,0:T(2,128)(2,1)} %spatial.1), calls=%async_computation | async-start | bytes 786432 | tf_op jit(solution)/shard_map/all_to_all | solution.py:169
  23.2 9.9 %collective-permute-start.2 = (bf16[24,192]{1,0:T(8,128)(2,1)S(1)}, bf16[24,192]{1,0:T(8,128)(2,1)S(1)}, u32[]{:S(2)}, u32[]{:S(2)}) collective-permute-start(bf16[24,192]{1,0:T(8,128)(2,1)S(1)} %get-tuple-element.13), channel_id=1, source_target_pairs={{0,2},{1,5},{2,0},{3,3},{4,6},{5,1},{6,4},{7,7},{8,10},{9,13},{10,... | collective-permute-start | bytes 27656 | tf_op jit(solution)/shard_map/ppermute | solution.py:144
  26.4 8.7 %collective-permute-start.1 = (bf16[24,192]{1,0:T(8,128)(2,1)S(1)}, bf16[24,192]{1,0:T(8,128)(2,1)S(1)}, u32[]{:S(2)}, u32[]{:S(2)}) collective-permute-start(bf16[24,192]{1,0:T(8,128)(2,1)S(1)} %get-tuple-element.14), channel_id=1, source_target_pairs={{0,1},{1,4},{2,7},{3,2},{4,5},{5,0},{6,3},{7,6},{8,9},{9,12},{10,1... | collective-permute-start | bytes 27656 | tf_op jit(solution)/shard_map/ppermute | solution.py:144
  32.4 2.7 %collective-permute-start = (bf16[24,192]{1,0:T(8,128)(2,1)S(1)}, bf16[24,192]{1,0:T(8,128)(2,1)S(1)}, u32[]{:S(2)}, u32[]{:S(2)}) collective-permute-start(bf16[24,192]{1,0:T(8,128)(2,1)S(1)} %get-tuple-element.12), channel_id=1, source_target_pairs={{0,0},{1,3},{2,6},{3,1},{4,4},{5,7},{6,2},{7,5},{8,8},{9,11},{10,1... | collective-permute-start | bytes 27656 | tf_op jit(solution)/shard_map/ppermute | solution.py:144
  52.4 63.9 %all-to-all-start.1 = ((bf16[4,128,1536]{2,1,0:T(8,128)(2,1)}), bf16[4,128,1536]{2,1,0:T(8,128)(2,1)}, u32[]{:S(2)}, u32[]{:S(2)}) async-start(bf16[4,128,1536]{2,1,0:T(8,128)(2,1)} %broadcast_in_dim.8), calls=%async_computation.1 | async-start | bytes 3145728 | tf_op jit(solution)/shard_map/all_to_all | solution.py:136
  81.1 18.6 %collective-permute-start.4 = (bf16[16,24,576]{2,1,0:T(8,128)(2,1)S(1)}, bf16[16,24,576]{2,1,0:T(8,128)(2,1)S(1)}, u32[]{:S(2)}, u32[]{:S(2)}) collective-permute-start(bf16[16,24,576]{2,1,0:T(8,128)(2,1)S(1)} %bitcast.18), channel_id=1, source_target_pairs={{0,16},{16,1},{1,17},{17,0},{2,18},{18,3},{3,19},{19,2},{4,20},{20... | collective-permute-start | bytes 1327112 | tf_op jit(solution)/shard_map/ppermute | solution.py:158
  83.0 27.3 %collective-permute-start.6 = (bf16[16,24,576]{2,1,0:T(8,128)(2,1)S(1)}, bf16[16,24,576]{2,1,0:T(8,128)(2,1)S(1)}, u32[]{:S(2)}, u32[]{:S(2)}) collective-permute-start(bf16[16,24,576]{2,1,0:T(8,128)(2,1)S(1)} %bitcast.19), channel_id=1, source_target_pairs={{0,1},{16,17},{1,0},{17,16},{2,3},{18,19},{3,2},{19,18},{4,5},{20,... | collective-permute-start | bytes 1327112 | tf_op jit(solution)/shard_map/ppermute | solution.py:158
  87.4 24.8 %collective-permute-start.8 = (bf16[16,24,576]{2,1,0:T(8,128)(2,1)S(1)}, bf16[16,24,576]{2,1,0:T(8,128)(2,1)S(1)}, u32[]{:S(2)}, u32[]{:S(2)}) collective-permute-start(bf16[16,24,576]{2,1,0:T(8,128)(2,1)S(1)} %bitcast.20), channel_id=1, source_target_pairs={{0,17},{16,0},{1,16},{17,1},{2,19},{18,2},{3,18},{19,3},{4,21},{20... | collective-permute-start | bytes 1327112 | tf_op jit(solution)/shard_map/ppermute | solution.py:158
  91.4 23.3 %collective-permute-start.3 = (bf16[16,24,576]{2,1,0:T(8,128)(2,1)S(1)}, bf16[16,24,576]{2,1,0:T(8,128)(2,1)S(1)}, u32[]{:S(2)}, u32[]{:S(2)}) collective-permute-start(bf16[16,24,576]{2,1,0:T(8,128)(2,1)S(1)} %bitcast.21), channel_id=1, source_target_pairs={{0,8},{8,0},{1,9},{9,1},{2,10},{10,2},{3,11},{11,3},{4,12},{12,4},... | collective-permute-start | bytes 1327112 | tf_op jit(solution)/shard_map/ppermute | solution.py:159
  99.7 15.0 %collective-permute-start.5 = (bf16[16,24,576]{2,1,0:T(8,128)(2,1)S(1)}, bf16[16,24,576]{2,1,0:T(8,128)(2,1)S(1)}, u32[]{:S(2)}, u32[]{:S(2)}) collective-permute-start(bf16[16,24,576]{2,1,0:T(8,128)(2,1)S(1)} %collective-permute-done.4.refs_2_), channel_id=1, source_target_pairs={{0,8},{8,0},{1,9},{9,1},{2,10},{10,2},{3,11},{11,3},{4,12},{12,4},... | collective-permute-start | bytes 1327112 | tf_op jit(solution)/shard_map/ppermute | solution.py:159
  110.3 4.4 %collective-permute-start.7 = (bf16[16,24,576]{2,1,0:T(8,128)(2,1)S(1)}, bf16[16,24,576]{2,1,0:T(8,128)(2,1)S(1)}, u32[]{:S(2)}, u32[]{:S(2)}) collective-permute-start(bf16[16,24,576]{2,1,0:T(8,128)(2,1)S(1)} %collective-permute-done.6.refs_4_), channel_id=1, source_target_pairs={{0,8},{8,0},{1,9},{9,1},{2,10},{10,2},{3,11},{11,3},{4,12},{12,4},... | collective-permute-start | bytes 1327112 | tf_op jit(solution)/shard_map/ppermute | solution.py:159
  112.2 4.0 %copy-start.1 = (bf16[16,24,576]{2,1,0:T(8,128)(2,1)}, bf16[16,24,576]{2,1,0:T(8,128)(2,1)S(1)}, u32[]{:S(2)}) copy-start(bf16[16,24,576]{2,1,0:T(8,128)(2,1)S(1)} %collective-permute-done.8.refs_6_) | copy-start | bytes 1327108
  112.3 4.0 %collective-permute-start.9 = (bf16[16,24,576]{2,1,0:T(8,128)(2,1)S(1)}, bf16[16,24,576]{2,1,0:T(8,128)(2,1)}, u32[]{:S(2)}, u32[]{:S(2)}) collective-permute-start(bf16[16,24,576]{2,1,0:T(8,128)(2,1)S(1)} %collective-permute-done.8.refs_6_), channel_id=1, source_target_pairs={{0,8},{8,0},{1,9},{9,1},{2,10},{10,2},{3,11},{11,3},{4,12},{12,4},... | collective-permute-start | bytes 1327112 | tf_op jit(solution)/shard_map/ppermute | solution.py:159
  114.7 0.8 copy-start.2
